TPU v7x, 32 devices: a whole 2x2x4 slice. The times are simulated.
32 devices in a mesh: vocab: 8 (over y, x, core), blk: 4 (over z).
Axes of the slice: x: 2, y: 2, z: 4, core: 2. Of those that a mesh axis runs over, the one named last changes fastest.
Arguments:
- char_ids: int32 [16384, 50], P(('vocab', 'blk')), may hold values from 0 to 255, as said below
- char_table: bfloat16 [256, 16], replicated, may hold values from -5 to 5
- conv_weight: bfloat16 [112, 896], replicated, may hold values from -0.75 to 0.75
- proj_weight: bfloat16 [896, 1024], replicated, may hold values from -0.1875 to 0.1875
- gate_weight: bfloat16 [2, 1024, 1024], replicated, may hold values from -0.1875 to 0.1875
- trans_weight: bfloat16 [2, 1024, 1024], replicated, may hold values from -0.1875 to 0.1875
- gate_bias: float32 [2, 1024], replicated, may hold values from -4 to 4
- hidden: bfloat16 [2048, 1024], P(('vocab', 'blk')), may hold values from -48 to 48
- targets: int32 [2048], P(('vocab', 'blk')), may hold values from 0 to 16383
Outputs:
- row_loss: float32 [2048], P(('vocab', 'blk'))
- hidden_grad: bfloat16 [2048, 1024], P(('vocab', 'blk'))
Inputs may be any that keep to these rules, and one draw needn't show every extreme that they name: `char_ids`: each word has 2 to 50 characters with ids 1 and up, followed by the padding id 0.
All inputs are finite; a program needn't handle non-finite values.
Results may differ from a plain program's by a relative error of at most 0.014.
The roundings to bfloat16 on the way count: a program that leaves them out, or rounds other values in their place, can miss the bound.
Values may be sent and summed in bfloat16 or wider, within the bound.
No kernel may reach another device: no remote copies, remote signals or barrier semaphores. Data moves between devices by JAX's collectives and lax.ppermute only.
A program may use at most 128 MiB of HBM per device.

v0:
```python
import math
import jax
import jax.numpy as jnp
from jax import lax
from jax.sharding import PartitionSpec as P


def shifted(array, axis, by):
    count = lax.axis_size(axis)
    return lax.ppermute(array, axis, [(i, (i + by) % count) for i in range(count)])


def char_features(char_ids, char_table, conv_weight):
    num_words = char_ids.shape[0]
    length = char_ids.shape[1]
    symbols = char_table.shape[0]
    embed_dim = char_table.shape[1]
    widths = conv_weight.shape[0] // embed_dim
    filters = conv_weight.shape[1] // widths
    onehot = (char_ids[:, :, None] == jnp.arange(symbols, dtype=jnp.int32)[None, None, :]).astype(
        jnp.bfloat16
    )
    vectors = jnp.dot(
        onehot.reshape(num_words * length, symbols), char_table, preferred_element_type=jnp.float32
    )
    vectors = vectors.astype(jnp.bfloat16).reshape(num_words, length, embed_dim)
    padded = jnp.pad(vectors, ((0, 0), (0, widths - 1), (0, 0)))
    windows = jnp.concatenate(
        [padded[:, shift_at : shift_at + length, :] for shift_at in range(widths)], axis=2
    )
    offset = jnp.arange(widths * embed_dim) // embed_dim
    kernel = jnp.arange(widths * filters) // filters + 1
    masked = jnp.where(offset[:, None] < kernel[None, :], conv_weight, jnp.zeros_like(conv_weight))
    conv_out = jnp.dot(
        windows.reshape(num_words * length, widths * embed_dim),
        masked,
        preferred_element_type=jnp.float32,
    )
    conv_out = conv_out.reshape(num_words, length, widths * filters)
    position = jnp.arange(length)
    usable = position[:, None] <= length - kernel[None, :]
    pooled = jnp.max(jnp.where(usable[None, :, :], conv_out, -jnp.inf), axis=1)
    return jnp.tanh(pooled).astype(jnp.bfloat16)


def embed_words(
    char_ids, char_table, conv_weight, proj_weight, gate_weight, trans_weight, gate_bias
):
    features = char_features(char_ids, char_table, conv_weight)
    current = jnp.dot(features, proj_weight, preferred_element_type=jnp.float32).astype(
        jnp.bfloat16
    )
    for layer_idx in range(gate_weight.shape[0]):
        opened = jax.nn.sigmoid(
            jnp.dot(current, gate_weight[layer_idx], preferred_element_type=jnp.float32)
            + gate_bias[layer_idx]
        )
        carried = jax.nn.relu(
            jnp.dot(current, trans_weight[layer_idx], preferred_element_type=jnp.float32)
        )
        current = (opened * carried + (1.0 - opened) * current.astype(jnp.float32)).astype(
            jnp.bfloat16
        )
    return current


def embed_all(char_ids, char_table, conv_weight, proj_weight, gate_weight, trans_weight, gate_bias):
    num_total = char_ids.shape[0]
    block_size = math.gcd(num_total, 128)
    grouped = char_ids.reshape(num_total // block_size, block_size, char_ids.shape[1])

    def one_block(piece_ids):
        return embed_words(
            piece_ids, char_table, conv_weight, proj_weight, gate_weight, trans_weight, gate_bias
        )

    return lax.map(one_block, grouped).reshape(num_total, proj_weight.shape[1])


def pick_targets(word_panel, row_spot):
    count_words = word_panel.shape[0]
    inside = (row_spot >= 0) & (row_spot < count_words)
    picked = jnp.take(word_panel, jnp.clip(row_spot, 0, count_words - 1), axis=0).astype(
        jnp.float32
    )
    return jnp.where(inside[:, None], picked, jnp.zeros_like(picked))


def fold_panel(acc_state, row_block, row_spot, word_panel):
    run_max, run_total, weighted, target_vec = acc_state
    scores = lax.dot_general(
        row_block, word_panel, (((1,), (1,)), ((), ())), preferred_element_type=jnp.float32
    )
    new_max = jnp.maximum(run_max, jnp.max(scores, axis=1))
    rescale = jnp.exp(run_max - new_max)
    soft_weights = jnp.exp(scores - new_max[:, None]).astype(jnp.bfloat16)
    run_total = run_total * rescale + jnp.sum(soft_weights.astype(jnp.float32), axis=1)
    weighted = weighted * rescale[:, None] + jnp.dot(
        soft_weights, word_panel, preferred_element_type=jnp.float32
    )
    target_vec = target_vec + pick_targets(word_panel, row_spot)
    return (new_max, run_total, weighted, target_vec)


def finish_rows(hidden, run_max, run_total, weighted, target_vec):
    target_score = jnp.sum(hidden.astype(jnp.float32) * target_vec, axis=1)
    row_loss = run_max + jnp.log(run_total) - target_score
    hidden_grad = (weighted / run_total[:, None] - target_vec).astype(jnp.bfloat16)
    return (row_loss, hidden_grad)


def per_device(
    char_ids,
    char_table,
    conv_weight,
    proj_weight,
    gate_weight,
    trans_weight,
    gate_bias,
    hidden,
    targets,
):
    embeds = embed_all(
        char_ids, char_table, conv_weight, proj_weight, gate_weight, trans_weight, gate_bias
    )
    local_words = embeds.shape[0]
    my_rows = hidden.shape[0]
    model_dim = hidden.shape[1]
    blocks = lax.axis_size("blk")
    group_idx = lax.axis_index("blk")
    word_panel = lax.all_gather(embeds, "vocab", axis=0, tiled=True)
    group_hidden = lax.all_gather(hidden, "blk", axis=0, tiled=True)
    group_goal = lax.all_gather(targets, "blk", axis=0, tiled=True)
    owner_dev = group_goal // local_words
    in_group = owner_dev % blocks == group_idx
    spot_all = jnp.where(in_group, owner_dev // blocks * local_words + group_goal % local_words, -1)
    running = (
        jnp.full((my_rows,), -jnp.inf, jnp.float32),
        jnp.zeros((my_rows,), jnp.float32),
        jnp.zeros((my_rows, model_dim), jnp.float32),
        jnp.zeros((my_rows, model_dim), jnp.float32),
    )
    for step_idx in range(blocks):
        which_block = (group_idx - step_idx) % blocks
        row_block = lax.dynamic_slice_in_dim(group_hidden, which_block * my_rows, my_rows, 0)
        row_spot = lax.dynamic_slice_in_dim(spot_all, which_block * my_rows, my_rows, 0)
        running = fold_panel(running, row_block, row_spot, word_panel)
        running = shifted((running[0], running[1], running[2], running[3]), "blk", 1)
    run_max, run_total, weighted, target_vec = running
    return finish_rows(hidden, run_max, run_total, weighted, target_vec)


def solution(mesh):
    return jax.shard_map(
        per_device,
        mesh=mesh,
        in_specs=(
            P(("vocab", "blk"), None),
            P(),
            P(),
            P(),
            P(),
            P(),
            P(),
            P(("vocab", "blk"), None),
            P(("vocab", "blk")),
        ),
        out_specs=(P(("vocab", "blk")), P(("vocab", "blk"), None)),
        check_vma=False,
    )
```

profile of v0, /device:TPU:0, one launch (start us, length us, event | category | flops | bytes accessed | tf_op | source)
XLA Modules:
  0.0 273.5 jit_solution(3712595097836582395)
XLA Ops:
  7.2 1.0 copy.20
  8.3 100.8 %while.13 = (s32[]{:T(128)}, bf16[4,128,1024]{2,1,0:T(8,128)(2,1)}, s32[4,128,50]{2,1,0:T(8,128)S(1)}, bf16[256,16]{0,1:T(8,128)(2,1)}, bf16[112,896]{1,0:T(8,12...) while((s32[]{:T(128)}, bf16[4,128,1024]{2,1,0:T(8,128)(2,1)}, ...), condition=%wide.region_2.3_spmd, body=%wide.region_0.2_spmd.sunk | while | flops 2662044928 | bytes 67010176 | solution.py:77
  8.5 4.2 %convolution_convert_fusion.4 = bf16[6400,16]{0,1:T(8,128)(2,1)S(1)} fusion(bf16[256,16]{0,1:T(8,128)(2,1)} %get-tuple-element.308, s32[6400]{0:T(1024)S(1)} %eq.53), kind=kOutput, calls=%fused_computation.5.clone.1 | convolution fusion | flops 54169600 | bytes 238592 | tf_op jit(solution)/shard_map/while/body/eval_jaxpr/dot_general | solution.py:23
  12.7 1.5 concatenate.12
  15.2 1.7 pad_slice_fusion.7
  16.9 1.4 copy.29
  23.4 0.8 constant_dynamic-update-slice_fusion.20
  24.2 4.8 %select_reduce_fusion.2 = f32[128,896]{1,0:T(8,128)S(1)} fusion(pred[50,896]{1,0:T(8,128)(4,1)S(1)} %iota_compare_fusion.6, bf16[128,50,112]{0,2,1:T(8,128)(2,1)} %constant_dynamic-update-slice_fusion.20, bf16[112,896]{1,0:T(8,128)(2,1)S(1)} %copy-done.9, s32[896]{0:T(1024)S(1)} %fusion.150, s32[112]{0:T(128)S(1)} %and_select_fusion.6), kind=kOutput, calls=%fused_computation.4.clone.1 | convolution fusion | flops 1296060416 | bytes 2141888 | tf_op jit(solution)/shard_map/while/body/eval_jaxpr/dot_general | solution.py:34
  30.0 1.2 copy-done.8
  32.2 1.2 fusion.155
  33.7 4.2 %convolution_convert_fusion.4 = bf16[6400,16]{0,1:T(8,128)(2,1)S(1)} fusion(bf16[256,16]{0,1:T(8,128)(2,1)} %get-tuple-element.308, s32[6400]{0:T(1024)S(1)} %eq.53), kind=kOutput, calls=%fused_computation.5.clone.1 | convolution fusion | flops 54169600 | bytes 238592 | tf_op jit(solution)/shard_map/while/body/eval_jaxpr/dot_general | solution.py:23
  37.9 1.5 concatenate.12
  40.4 1.7 pad_slice_fusion.7
  42.0 1.4 copy.29
  48.5 0.8 constant_dynamic-update-slice_fusion.20
  49.4 4.8 %select_reduce_fusion.2 = f32[128,896]{1,0:T(8,128)S(1)} fusion(pred[50,896]{1,0:T(8,128)(4,1)S(1)} %iota_compare_fusion.6, bf16[128,50,112]{0,2,1:T(8,128)(2,1)} %constant_dynamic-update-slice_fusion.20, bf16[112,896]{1,0:T(8,128)(2,1)S(1)} %copy-done.9, s32[896]{0:T(1024)S(1)} %fusion.150, s32[112]{0:T(128)S(1)} %and_select_fusion.6), kind=kOutput, calls=%fused_computation.4.clone.1 | convolution fusion | flops 1296060416 | bytes 2141888 | tf_op jit(solution)/shard_map/while/body/eval_jaxpr/dot_general | solution.py:34
  55.2 1.2 copy-done.8
  57.4 1.2 fusion.155
  58.9 4.2 %convolution_convert_fusion.4 = bf16[6400,16]{0,1:T(8,128)(2,1)S(1)} fusion(bf16[256,16]{0,1:T(8,128)(2,1)} %get-tuple-element.308, s32[6400]{0:T(1024)S(1)} %eq.53), kind=kOutput, calls=%fused_computation.5.clone.1 | convolution fusion | flops 54169600 | bytes 238592 | tf_op jit(solution)/shard_map/while/body/eval_jaxpr/dot_general | solution.py:23
  63.1 1.5 concatenate.12
  65.6 1.7 pad_slice_fusion.7
  67.2 1.4 copy.29
  74.6 4.8 %select_reduce_fusion.2 = f32[128,896]{1,0:T(8,128)S(1)} fusion(pred[50,896]{1,0:T(8,128)(4,1)S(1)} %iota_compare_fusion.6, bf16[128,50,112]{0,2,1:T(8,128)(2,1)} %constant_dynamic-update-slice_fusion.20, bf16[112,896]{1,0:T(8,128)(2,1)S(1)} %copy-done.9, s32[896]{0:T(1024)S(1)} %fusion.150, s32[112]{0:T(128)S(1)} %and_select_fusion.6), kind=kOutput, calls=%fused_computation.4.clone.1 | convolution fusion | flops 1296060416 | bytes 2141888 | tf_op jit(solution)/shard_map/while/body/eval_jaxpr/dot_general | solution.py:34
  80.4 1.2 copy-done.8
  82.6 1.2 fusion.155
  84.1 4.2 %convolution_convert_fusion.4 = bf16[6400,16]{0,1:T(8,128)(2,1)S(1)} fusion(bf16[256,16]{0,1:T(8,128)(2,1)} %get-tuple-element.308, s32[6400]{0:T(1024)S(1)} %eq.53), kind=kOutput, calls=%fused_computation.5.clone.1 | convolution fusion | flops 54169600 | bytes 238592 | tf_op jit(solution)/shard_map/while/body/eval_jaxpr/dot_general | solution.py:23
  88.3 1.5 concatenate.12
  90.8 1.7 pad_slice_fusion.7
  92.4 1.4 copy.29
  99.8 4.8 %select_reduce_fusion.2 = f32[128,896]{1,0:T(8,128)S(1)} fusion(pred[50,896]{1,0:T(8,128)(4,1)S(1)} %iota_compare_fusion.6, bf16[128,50,112]{0,2,1:T(8,128)(2,1)} %constant_dynamic-update-slice_fusion.20, bf16[112,896]{1,0:T(8,128)(2,1)S(1)} %copy-done.9, s32[896]{0:T(1024)S(1)} %fusion.150, s32[112]{0:T(128)S(1)} %and_select_fusion.6), kind=kOutput, calls=%fused_computation.4.clone.1 | convolution fusion | flops 1296060416 | bytes 2141888 | tf_op jit(solution)/shard_map/while/body/eval_jaxpr/dot_general | solution.py:34
  105.6 1.2 copy-done.8
  107.8 1.2 fusion.155
  110.7 9.9 %all-reduce.1 = s32[256]{0:T(256)S(1)} all-reduce(s32[256]{0:T(256)S(1)} %dynamic-update-slice), channel_id=1, replica_groups=mesh['vocab'=8,'blk'=4] {'blk'}, use_global_device_ids=true, to_apply=%add.1 | all-reduce | flops 256 | bytes 2048
  121.3 15.9 %all_gather.9 = bf16[256,1024]{1,0:T(8,128)(2,1)S(1)} all-gather(bf16[64,1024]{1,0:T(8,128)(2,1)} %param.20), channel_id=1, replica_groups=mesh['vocab'=8,'blk'=4] {'blk'}, dimensions={0}, use_global_device_ids=true | all-gather | bytes 655360 | tf_op jit(solution)/shard_map/all_gather | solution.py:132
  137.3 29.1 %all-gather.2.cloned.1.call-done = bf16[4096,1024]{1,0:T(8,128)(2,1)} async-done(((bf16[512,1024]{1,0:T(8,128)(2,1)}), bf16[4096,1024]{1,0:T(8,128)(2,1)}) %all-gather.2.cloned.1.call-update) | async-done | bytes 8388624 | tf_op jit(solution)/shard_map/all_gather | solution.py:131
  166.3 5.3 %gather_fusion = bf16[64,1024]{1,0:T(8,128)(2,1)S(1)} fusion(bf16[4096,1024]{1,0:T(8,128)(2,1)} %all-gather.2.cloned.1.call-done, s32[1024]{0:T(1024)S(1)} %pad_clamp_fusion.3), kind=kCustom, calls=%fused_computation.clone | custom fusion | bytes 262400 | tf_op jit(solution)/shard_map/jit(_take)/gather | solution.py:83
  171.6 0.8 convert_select_fusion
  172.4 1.5 collective-permute-start.8
  173.9 6.7 %fusion.101 = (f32[64]{0:T(128)S(1)}, f32[64,4096]{1,0:T(8,128)S(1)}) fusion(bf16[4096,1024]{1,0:T(8,128)(2,1)} %all-gather.2.cloned.1.call-done, bf16[256,1024]{1,0:T(8,128)(2,1)S(1)} %all_gather.9, s32[]{:T(128)S(6)} %select_n.128), kind=kOutput, calls=%fused_computation.147 | convolution fusion | flops 537132992 | bytes 9568516 | tf_op jit(solution)/shard_map/dot_general | solution.py:91
  180.6 1.5 collective-permute-start
  183.1 2.4 convolution_add_fusion
  185.5 1.5 collective-permute-start.12
  187.1 3.3 %fusion.102 = (f32[64]{0:T(128)}, f32[64,4096]{1,0:T(8,128)S(1)}) fusion(bf16[4096,1024]{1,0:T(8,128)(2,1)S(1)} %copy-done, bf16[256,1024]{1,0:T(8,128)(2,1)S(1)} %all_gather.9, s32[]{:T(128)S(6)} %select_n.130), kind=kOutput, calls=%fused_computation.148 | convolution fusion | flops 537132992 | bytes 9568516 | tf_op jit(solution)/shard_map/dot_general | solution.py:91
  190.4 3.3 %fusion.103 = (f32[64]{0:T(128)}, f32[64,4096]{1,0:T(8,128)S(1)}) fusion(bf16[4096,1024]{1,0:T(8,128)(2,1)S(1)} %copy-done, bf16[256,1024]{1,0:T(8,128)(2,1)S(1)} %all_gather.9, s32[]{:T(128)S(6)} %select_n.132), kind=kOutput, calls=%fused_computation.149 | convolution fusion | flops 537132992 | bytes 9568516 | tf_op jit(solution)/shard_map/dot_general | solution.py:91
  193.6 4.2 %fusion.104 = (f32[64]{0:T(128)}, f32[64,4096]{1,0:T(8,128)S(1)}) fusion(bf16[4096,1024]{1,0:T(8,128)(2,1)S(1)} %copy-done, bf16[256,1024]{1,0:T(8,128)(2,1)} %copy-done.2, s32[]{:T(128)S(6)} %select_n.134), kind=kOutput, calls=%fused_computation.150 | convolution fusion | flops 537132992 | bytes 9568516 | tf_op jit(solution)/shard_map/dot_general | solution.py:91
  197.8 5.3 %gather_fusion.1 = bf16[64,1024]{1,0:T(8,128)(2,1)S(1)} fusion(bf16[4096,1024]{1,0:T(8,128)(2,1)} %all-gather.2.cloned.1.call-done, s32[1024]{0:T(1024)S(1)} %pad_clamp_fusion.2), kind=kCustom, calls=%fused_computation.1.clone | custom fusion | bytes 262400 | tf_op jit(solution)/shard_map/jit(_take)/gather | solution.py:83
  203.0 5.3 %gather_fusion.2 = bf16[64,1024]{1,0:T(8,128)(2,1)S(1)} fusion(bf16[4096,1024]{1,0:T(8,128)(2,1)} %all-gather.2.cloned.1.call-done, s32[1024]{0:T(1024)S(1)} %pad_clamp_fusion.1), kind=kCustom, calls=%fused_computation.2.clone | custom fusion | bytes 262400 | tf_op jit(solution)/shard_map/jit(_take)/gather | solution.py:83
  208.3 5.3 %gather_fusion.3 = bf16[64,1024]{1,0:T(8,128)(2,1)S(1)} fusion(bf16[4096,1024]{1,0:T(8,128)(2,1)} %all-gather.2.cloned.1.call-done, s32[1024]{0:T(1024)S(1)} %pad_clamp_fusion), kind=kCustom, calls=%fused_computation.3.clone | custom fusion | bytes 262400 | tf_op jit(solution)/shard_map/jit(_take)/gather | solution.py:83
  214.2 1.9 collective-permute-start.1
  217.0 1.5 collective-permute-start.5
  218.5 1.0 collective-permute-done.1
  221.0 1.4 collective-permute-done.5
  222.4 3.1 %collective-permute-done.2 = f32[64]{0:T(128)S(1)} collective-permute-done((f32[64]{0:T(128)S(1)}, f32[64]{0:T(128)S(1)}, u32[]{:S(2)}, u32[]{:S(2)}) %collective-permute-start.2) | collective-permute-done | bytes 288 | tf_op jit(solution)/shard_map/ppermute | solution.py:10
  226.1 1.1 select_add_fusion.2
  227.5 5.2 %multiply_add_fusion.2 = f32[64,1024]{1,0:T(8,128)S(1)} fusion(f32[64,1024]{1,0:T(8,128)} %collective-permute-done.12, f32[64]{0:T(128)S(1)} %get-tuple-element.173, bf16[4096,1024]{1,0:T(8,128)(2,1)} %all-gather.2.cloned.1.call-done, f32[64,4096]{1,0:T(8,128)S(1)} %get-tuple-element.209, f32[64]{0:T(128)S(1)} %max.43), kind=kOutput, calls=%fused_computation.88 | convolution fusion | flops 537526272 | bytes 9961984 | tf_op jit(solution)/shard_map/dot_general | solution.py:98
  233.0 4.1 %collective-permute-done.9 = f32[64,1024]{1,0:T(8,128)S(1)} collective-permute-done((f32[64,1024]{1,0:T(8,128)S(1)}, f32[64,1024]{1,0:T(8,128)S(1)}, u32[]{:S(2)}, u32[]{:S(2)}) %collective-permute-start.9) | collective-permute-done | bytes 262176 | tf_op jit(solution)/shard_map/ppermute | solution.py:10
  237.3 6.5 %collective-permute-done.13 = f32[64,1024]{1,0:T(8,128)S(1)} collective-permute-done((f32[64,1024]{1,0:T(8,128)S(1)}, f32[64,1024]{1,0:T(8,128)S(1)}, u32[]{:S(2)}, u32[]{:S(2)}) %collective-permute-start.13) | collective-permute-done | bytes 262176 | tf_op jit(solution)/shard_map/ppermute | solution.py:10
  243.7 1.7 multiply_add_fusion.1
  245.5 3.1 %collective-permute-done.10 = f32[64,1024]{1,0:T(8,128)S(1)} collective-permute-done((f32[64,1024]{1,0:T(8,128)S(1)}, f32[64,1024]{1,0:T(8,128)S(1)}, u32[]{:S(2)}, u32[]{:S(2)}) %collective-permute-start.10) | collective-permute-done | bytes 262176 | tf_op jit(solution)/shard_map/ppermute | solution.py:10
  248.8 6.4 %collective-permute-done.14 = f32[64,1024]{1,0:T(8,128)S(1)} collective-permute-done((f32[64,1024]{1,0:T(8,128)S(1)}, f32[64,1024]{1,0:T(8,128)S(1)}, u32[]{:S(2)}, u32[]{:S(2)}) %collective-permute-start.14) | collective-permute-done | bytes 262176 | tf_op jit(solution)/shard_map/ppermute | solution.py:10
  255.2 1.7 multiply_add_fusion
  257.2 2.5 collective-permute-start.3
  259.7 5.6 %collective-permute-done.7 = f32[64]{0:T(128)S(1)} collective-permute-done((f32[64]{0:T(128)S(1)}, f32[64]{0:T(128)S(1)}, u32[]{:S(2)}, u32[]{:S(2)}) %collective-permute-start.7) | collective-permute-done | bytes 288 | tf_op jit(solution)/shard_map/ppermute | solution.py:10
  265.2 0.9 subtract_convert_fusion
  (193 shorter events, 43.0 us)
Async XLA Ops:
  7.2 159.2 %all-gather.2.cloned.1.call-start = ((), (), s32[]{:S(2)}) async-start(), calls=%async_computation | async-start | bytes 9437184 | tf_op jit(solution)/shard_map/all_gather | solution.py:131
  8.2 100.9 %copy-start.11 = (u32[32]{0:T(128)S(1)}, u32[32]{0:T(128)}, u32[]{:S(2)}) copy-start(u32[32]{0:T(128)} %constant.224) | copy-start | bytes 388
  8.3 102.2 %copy-start.10 = (s32[64]{0:T(128)S(1)}, s32[64]{0:T(128)}, u32[]{:S(2)}) copy-start(s32[64]{0:T(128)} %param.21) | copy-start | bytes 772
  16.9 7.3 %copy-start.9 = (bf16[112,896]{1,0:T(8,128)(2,1)S(1)}, bf16[112,896]{1,0:T(8,128)(2,1)}, u32[]{:S(2)}) copy-start(bf16[112,896]{1,0:T(8,128)(2,1)} %get-tuple-element.309) | copy-start | bytes 602116 | tf_op jit(solution)/shard_map/while
  24.1 4.9 %copy-start.1 = (bf16[896,1024]{1,0:T(8,128)(2,1)S(1)}, bf16[896,1024]{1,0:T(8,128)(2,1)}, u32[]{:S(2)}) copy-start(bf16[896,1024]{1,0:T(8,128)(2,1)} %get-tuple-element.310) | copy-start | bytes 5505028 | tf_op jit(solution)/shard_map/while
  24.2 5.3 %copy-start.4 = (f32[2,1024]{1,0:T(2,128)S(1)}, f32[2,1024]{1,0:T(2,128)}, u32[]{:S(2)}) copy-start(f32[2,1024]{1,0:T(2,128)} %get-tuple-element.312) | copy-start | bytes 24580 | tf_op jit(solution)/shard_map/while
  24.2 5.3 %copy-start.7 = (bf16[2,1024,1024]{2,1,0:T(8,128)(2,1)S(1)}, bf16[2,1024,1024]{2,1,0:T(8,128)(2,1)}, u32[]{:S(2)}) copy-start(bf16[2,1024,1024]{2,1,0:T(8,128)(2,1)} %get-tuple-element.311) | copy-start | bytes 12582916 | tf_op jit(solution)/shard_map/while
  29.0 2.2 copy-start.8
  42.0 7.3 %copy-start.9 = (bf16[112,896]{1,0:T(8,128)(2,1)S(1)}, bf16[112,896]{1,0:T(8,128)(2,1)}, u32[]{:S(2)}) copy-start(bf16[112,896]{1,0:T(8,128)(2,1)} %get-tuple-element.309) | copy-start | bytes 602116 | tf_op jit(solution)/shard_map/while
  49.3 4.9 %copy-start.1 = (bf16[896,1024]{1,0:T(8,128)(2,1)S(1)}, bf16[896,1024]{1,0:T(8,128)(2,1)}, u32[]{:S(2)}) copy-start(bf16[896,1024]{1,0:T(8,128)(2,1)} %get-tuple-element.310) | copy-start | bytes 5505028 | tf_op jit(solution)/shard_map/while
  49.3 5.3 %copy-start.4 = (f32[2,1024]{1,0:T(2,128)S(1)}, f32[2,1024]{1,0:T(2,128)}, u32[]{:S(2)}) copy-start(f32[2,1024]{1,0:T(2,128)} %get-tuple-element.312) | copy-start | bytes 24580 | tf_op jit(solution)/shard_map/while
  49.3 5.3 %copy-start.7 = (bf16[2,1024,1024]{2,1,0:T(8,128)(2,1)S(1)}, bf16[2,1024,1024]{2,1,0:T(8,128)(2,1)}, u32[]{:S(2)}) copy-start(bf16[2,1024,1024]{2,1,0:T(8,128)(2,1)} %get-tuple-element.311) | copy-start | bytes 12582916 | tf_op jit(solution)/shard_map/while
  54.2 2.2 copy-start.8
  67.2 7.3 %copy-start.9 = (bf16[112,896]{1,0:T(8,128)(2,1)S(1)}, bf16[112,896]{1,0:T(8,128)(2,1)}, u32[]{:S(2)}) copy-start(bf16[112,896]{1,0:T(8,128)(2,1)} %get-tuple-element.309) | copy-start | bytes 602116 | tf_op jit(solution)/shard_map/while
  74.5 4.9 %copy-start.1 = (bf16[896,1024]{1,0:T(8,128)(2,1)S(1)}, bf16[896,1024]{1,0:T(8,128)(2,1)}, u32[]{:S(2)}) copy-start(bf16[896,1024]{1,0:T(8,128)(2,1)} %get-tuple-element.310) | copy-start | bytes 5505028 | tf_op jit(solution)/shard_map/while
  74.5 5.3 %copy-start.4 = (f32[2,1024]{1,0:T(2,128)S(1)}, f32[2,1024]{1,0:T(2,128)}, u32[]{:S(2)}) copy-start(f32[2,1024]{1,0:T(2,128)} %get-tuple-element.312) | copy-start | bytes 24580 | tf_op jit(solution)/shard_map/while
  74.5 5.3 %copy-start.7 = (bf16[2,1024,1024]{2,1,0:T(8,128)(2,1)S(1)}, bf16[2,1024,1024]{2,1,0:T(8,128)(2,1)}, u32[]{:S(2)}) copy-start(bf16[2,1024,1024]{2,1,0:T(8,128)(2,1)} %get-tuple-element.311) | copy-start | bytes 12582916 | tf_op jit(solution)/shard_map/while
  79.4 2.2 copy-start.8
  92.4 7.3 %copy-start.9 = (bf16[112,896]{1,0:T(8,128)(2,1)S(1)}, bf16[112,896]{1,0:T(8,128)(2,1)}, u32[]{:S(2)}) copy-start(bf16[112,896]{1,0:T(8,128)(2,1)} %get-tuple-element.309) | copy-start | bytes 602116 | tf_op jit(solution)/shard_map/while
  99.7 4.9 %copy-start.1 = (bf16[896,1024]{1,0:T(8,128)(2,1)S(1)}, bf16[896,1024]{1,0:T(8,128)(2,1)}, u32[]{:S(2)}) copy-start(bf16[896,1024]{1,0:T(8,128)(2,1)} %get-tuple-element.310) | copy-start | bytes 5505028 | tf_op jit(solution)/shard_map/while
  99.7 5.3 %copy-start.4 = (f32[2,1024]{1,0:T(2,128)S(1)}, f32[2,1024]{1,0:T(2,128)}, u32[]{:S(2)}) copy-start(f32[2,1024]{1,0:T(2,128)} %get-tuple-element.312) | copy-start | bytes 24580 | tf_op jit(solution)/shard_map/while
  99.8 5.3 %copy-start.7 = (bf16[2,1024,1024]{2,1,0:T(8,128)(2,1)S(1)}, bf16[2,1024,1024]{2,1,0:T(8,128)(2,1)}, u32[]{:S(2)}) copy-start(bf16[2,1024,1024]{2,1,0:T(8,128)(2,1)} %get-tuple-element.311) | copy-start | bytes 12582916 | tf_op jit(solution)/shard_map/while
  104.6 2.2 copy-start.8
  137.3 53.1 %copy-start.2 = (bf16[256,1024]{1,0:T(8,128)(2,1)}, bf16[256,1024]{1,0:T(8,128)(2,1)S(1)}, u32[]{:S(2)}) copy-start(bf16[256,1024]{1,0:T(8,128)(2,1)S(1)} %all_gather.9) | copy-start | bytes 1572868
  172.4 10.7 %copy-start = (bf16[4096,1024]{1,0:T(8,128)(2,1)S(1)}, bf16[4096,1024]{1,0:T(8,128)(2,1)}, u32[]{:S(2)}) copy-start(bf16[4096,1024]{1,0:T(8,128)(2,1)} %all-gather.2.cloned.1.call-done) | copy-start | bytes 25165828
  172.4 53.7 %collective-permute-start.8 = (f32[64,1024]{1,0:T(8,128)}, f32[64,1024]{1,0:T(8,128)}, u32[]{:S(2)}, u32[]{:S(2)}) collective-permute-start(f32[64,1024]{1,0:T(8,128)} %convert_select_fusion), channel_id=1, source_target_pairs={{0,1},{1,2},{2,3},{3,0},{4,5},{5,6},{6,7},{7,4},{8,9},{9,10},{10,1... | collective-permute-start | bytes 786440 | tf_op jit(solution)/shard_map/ppermute | solution.py:10
  180.6 32.9 %collective-permute-start = (f32[64]{0:T(128)S(1)}, f32[64]{0:T(128)}, u32[]{:S(2)}, u32[]{:S(2)}) collective-permute-start(f32[64]{0:T(128)S(1)} %get-tuple-element.206), channel_id=1, source_target_pairs={{0,1},{1,2},{2,3},{3,0},{4,5},{5,6},{6,7},{7,4},{8,9},{9,10},{10,1... | collective-permute-start | bytes 776 | tf_op jit(solution)/shard_map/ppermute | solution.py:10
  185.5 41.9 %collective-permute-start.12 = (f32[64,1024]{1,0:T(8,128)}, f32[64,1024]{1,0:T(8,128)}, u32[]{:S(2)}, u32[]{:S(2)}) collective-permute-start(f32[64,1024]{1,0:T(8,128)} %convolution_add_fusion), channel_id=1, source_target_pairs={{0,1},{1,2},{2,3},{3,0},{4,5},{5,6},{6,7},{7,4},{8,9},{9,10},{10,1... | collective-permute-start | bytes 786440 | tf_op jit(solution)/shard_map/ppermute | solution.py:10
  187.0 29.4 %collective-permute-start.4 = (f32[64]{0:T(128)}, f32[64]{0:T(128)}, u32[]{:S(2)}, u32[]{:S(2)}) collective-permute-start(f32[64]{0:T(128)} %get-tuple-element.205), channel_id=1, source_target_pairs={{0,1},{1,2},{2,3},{3,0},{4,5},{5,6},{6,7},{7,4},{8,9},{9,10},{10,1... | collective-permute-start | bytes 776 | tf_op jit(solution)/shard_map/ppermute | solution.py:10
  214.2 5.3 %collective-permute-start.1 = (f32[64]{0:T(128)S(1)}, f32[64]{0:T(128)S(1)}, u32[]{:S(2)}, u32[]{:S(2)}) collective-permute-start(f32[64]{0:T(128)S(1)} %max.43), channel_id=1, source_target_pairs={{0,1},{1,2},{2,3},{3,0},{4,5},{5,6},{6,7},{7,4},{8,9},{9,10},{10,1... | collective-permute-start | bytes 776 | tf_op jit(solution)/shard_map/ppermute | solution.py:10
  217.0 5.3 %collective-permute-start.5 = (f32[64]{0:T(128)S(1)}, f32[64]{0:T(128)S(1)}, u32[]{:S(2)}, u32[]{:S(2)}) collective-permute-start(f32[64]{0:T(128)S(1)} %get-tuple-element.172), channel_id=1, source_target_pairs={{0,1},{1,2},{2,3},{3,0},{4,5},{5,6},{6,7},{7,4},{8,9},{9,10},{10,1... | collective-permute-start | bytes 776 | tf_op jit(solution)/shard_map/ppermute | solution.py:10
  220.2 5.3 %collective-permute-start.2 = (f32[64]{0:T(128)S(1)}, f32[64]{0:T(128)S(1)}, u32[]{:S(2)}, u32[]{:S(2)}) collective-permute-start(f32[64]{0:T(128)S(1)} %max.44), channel_id=1, source_target_pairs={{0,1},{1,2},{2,3},{3,0},{4,5},{5,6},{6,7},{7,4},{8,9},{9,10},{10,1... | collective-permute-start | bytes 776 | tf_op jit(solution)/shard_map/ppermute | solution.py:10
  220.6 23.1 %slice-start = ((s8[8388608]{0:T(1024)(128)(4,1)}), s8[4194304]{0:T(1024)(128)(4,1)S(1)}, s32[]{:S(2)}) async-start(s8[8388608]{0:T(1024)(128)(4,1)} %bitcast.111), calls=%async_computation.1 | async-start | bytes 8388608
  222.4 23.1 %collective-permute-start.6 = (f32[64]{0:T(128)S(1)}, f32[64]{0:T(128)S(1)}, u32[]{:S(2)}, u32[]{:S(2)}) collective-permute-start(f32[64]{0:T(128)S(1)} %get-tuple-element.170), channel_id=1, source_target_pairs={{0,1},{1,2},{2,3},{3,0},{4,5},{5,6},{6,7},{7,4},{8,9},{9,10},{10,1... | collective-permute-start | bytes 776 | tf_op jit(solution)/shard_map/ppermute | solution.py:10
  227.1 10.0 %collective-permute-start.9 = (f32[64,1024]{1,0:T(8,128)S(1)}, f32[64,1024]{1,0:T(8,128)S(1)}, u32[]{:S(2)}, u32[]{:S(2)}) collective-permute-start(f32[64,1024]{1,0:T(8,128)S(1)} %select_add_fusion.2), channel_id=1, source_target_pairs={{0,1},{1,2},{2,3},{3,0},{4,5},{5,6},{6,7},{7,4},{8,9},{9,10},{10,1... | collective-permute-start | bytes 786440 | tf_op jit(solution)/shard_map/ppermute | solution.py:10
  227.4 9.7 %copy-start.5 = (pred[64]{0:T(512)(128)(4,1)S(1)}, pred[64]{0:T(512)(128)(4,1)}, u32[]{:S(2)}) copy-start(pred[64]{0:T(512)(128)(4,1)} %get-tuple-element.195) | copy-start | bytes 196
  227.4 9.6 %copy-start.6 = (pred[64]{0:T(512)(128)(4,1)S(1)}, pred[64]{0:T(512)(128)(4,1)}, u32[]{:S(2)}) copy-start(pred[64]{0:T(512)(128)(4,1)} %get-tuple-element.198) | copy-start | bytes 196
  227.5 16.3 %slice-start.1 = ((s8[8388608]{0:T(1024)(128)(4,1)}), s8[4194304]{0:T(1024)(128)(4,1)S(1)}, s32[]{:S(2)}) async-start(s8[8388608]{0:T(1024)(128)(4,1)} %bitcast.111), calls=%async_computation.2 | async-start | bytes 8388608
  232.6 11.1 %collective-permute-start.13 = (f32[64,1024]{1,0:T(8,128)S(1)}, f32[64,1024]{1,0:T(8,128)S(1)}, u32[]{:S(2)}, u32[]{:S(2)}) collective-permute-start(f32[64,1024]{1,0:T(8,128)S(1)} %multiply_add_fusion.2), channel_id=1, source_target_pairs={{0,1},{1,2},{2,3},{3,0},{4,5},{5,6},{6,7},{7,4},{8,9},{9,10},{10,1... | collective-permute-start | bytes 786440 | tf_op jit(solution)/shard_map/ppermute | solution.py:10
  237.2 11.4 %collective-permute-start.10 = (f32[64,1024]{1,0:T(8,128)S(1)}, f32[64,1024]{1,0:T(8,128)S(1)}, u32[]{:S(2)}, u32[]{:S(2)}) collective-permute-start(f32[64,1024]{1,0:T(8,128)S(1)} %select_add_fusion.1), channel_id=1, source_target_pairs={{0,1},{1,2},{2,3},{3,0},{4,5},{5,6},{6,7},{7,4},{8,9},{9,10},{10,1... | collective-permute-start | bytes 786440 | tf_op jit(solution)/shard_map/ppermute | solution.py:10
  245.4 9.8 %collective-permute-start.14 = (f32[64,1024]{1,0:T(8,128)S(1)}, f32[64,1024]{1,0:T(8,128)S(1)}, u32[]{:S(2)}, u32[]{:S(2)}) collective-permute-start(f32[64,1024]{1,0:T(8,128)S(1)} %multiply_add_fusion.1), channel_id=1, source_target_pairs={{0,1},{1,2},{2,3},{3,0},{4,5},{5,6},{6,7},{7,4},{8,9},{9,10},{10,1... | collective-permute-start | bytes 786440 | tf_op jit(solution)/shard_map/ppermute | solution.py:10
  248.7 16.5 %collective-permute-start.11 = (f32[64,1024]{1,0:T(8,128)S(1)}, f32[64,1024]{1,0:T(8,128)S(1)}, u32[]{:S(2)}, u32[]{:S(2)}) collective-permute-start(f32[64,1024]{1,0:T(8,128)S(1)} %select_add_fusion), channel_id=1, source_target_pairs={{0,1},{1,2},{2,3},{3,0},{4,5},{5,6},{6,7},{7,4},{8,9},{9,10},{10,1... | collective-permute-start | bytes 786440 | tf_op jit(solution)/shard_map/ppermute | solution.py:10
  255.2 10.0 %copy-start.3 = (bf16[64,1024]{1,0:T(8,128)(2,1)S(1)}, bf16[64,1024]{1,0:T(8,128)(2,1)}, u32[]{:S(2)}) copy-start(bf16[64,1024]{1,0:T(8,128)(2,1)} %param.20) | copy-start | bytes 393220
  256.9 8.3 %collective-permute-start.15 = (f32[64,1024]{1,0:T(8,128)S(1)}, f32[64,1024]{1,0:T(8,128)S(1)}, u32[]{:S(2)}, u32[]{:S(2)}) collective-permute-start(f32[64,1024]{1,0:T(8,128)S(1)} %multiply_add_fusion), channel_id=1, source_target_pairs={{0,1},{1,2},{2,3},{3,0},{4,5},{5,6},{6,7},{7,4},{8,9},{9,10},{10,1... | collective-permute-start | bytes 786440 | tf_op jit(solution)/shard_map/ppermute | solution.py:10
  257.0 8.2 %collective-permute-start.7 = (f32[64]{0:T(128)S(1)}, f32[64]{0:T(128)S(1)}, u32[]{:S(2)}, u32[]{:S(2)}) collective-permute-start(f32[64]{0:T(128)S(1)} %get-tuple-element.168), channel_id=1, source_target_pairs={{0,1},{1,2},{2,3},{3,0},{4,5},{5,6},{6,7},{7,4},{8,9},{9,10},{10,1... | collective-permute-start | bytes 776 | tf_op jit(solution)/shard_map/ppermute | solution.py:10
  257.2 8.9 %collective-permute-start.3 = (f32[64]{0:T(128)S(1)}, f32[64]{0:T(128)S(1)}, u32[]{:S(2)}, u32[]{:S(2)}) collective-permute-start(f32[64]{0:T(128)S(1)} %max.45), channel_id=1, source_target_pairs={{0,1},{1,2},{2,3},{3,0},{4,5},{5,6},{6,7},{7,4},{8,9},{9,10},{10,1... | collective-permute-start | bytes 776 | tf_op jit(solution)/shard_map/ppermute | solution.py:10
Sparse Core Ops, SparseCore 0:
  109.2 57.0 all-gather.1
where the time goes:
time: 274 us; the launch traced here: 273 us
  matrix products  77.2 us (28%)
  local copies, waits for them, and re-layouts  74.1 us (27%)
  waiting for transfers between devices  60.3 us (22%)
  blocking collectives  25.8 us (9%)
  between operations  15.1 us (6%)
  starting transfers between devices  11.7 us (4%)
  other arithmetic  8.73 us (3%)
    ppermute x16, waiting for transfers between devices, shifted(): lax.ppermute(array, axis, [(i, (i + by) % count) for i in range(count)])  31.2 us
    all_gather x1, waiting for transfers between devices, per_device(): word_panel = lax.all_gather(embeds, 'vocab', axis=0, tiled=True)  29.1 us
    while x64, local copies, waits for them, and re-layouts  22.6 us
    gather x4, local copies, waits for them, and re-layouts, pick_targets(): jnp.take(word_panel, jnp.clip(row_spot, 0, count_words - 1), axis=0)  21 us
    dot_general x4, matrix products, char_features(): jnp.dot(windows.reshape(num_words * length, widths * embed_dim), masked,...  19.3 us
    slice x28, local copies, waits for them, and re-layouts, char_features(): padded[:, shift_at:shift_at + length, :]  17.8 us
    dot_general x4, matrix products, fold_panel(): lax.dot_general(row_block, word_panel, (((1,), (1,)), ((), ())), preferre...  17.4 us
    dot_general x4, matrix products, char_features(): jnp.dot(onehot.reshape(num_words * length, symbols), char_table, preferre...  16.7 us
  transfers between devices with their start and end apart: 17, of which 9 were waited for; matrix products, arithmetic and copies ran while one was open for 19% of the time, Pallas kernels for 0%

commit v1 on v0

--- a/solution.py
+++ b/solution.py
@@ -3,6 +3,12 @@
 import jax.numpy as jnp
 from jax import lax
 from jax.sharding import PartitionSpec as P
+
+
+def laid_out(blocks, dim):
+    shape = list(blocks.shape[1:])
+    shape[dim] *= blocks.shape[0]
+    return jnp.moveaxis(blocks, 0, dim).reshape(shape)
 
 
 def shifted(array, axis, by):
@@ -129,7 +135,19 @@
     blocks = lax.axis_size("blk")
     group_idx = lax.axis_index("blk")
     word_panel = lax.all_gather(embeds, "vocab", axis=0, tiled=True)
-    group_hidden = lax.all_gather(hidden, "blk", axis=0, tiled=True)
+    size = lax.axis_size("blk")
+    pairs = [(i_2, (i_2 + 1) % size) for i_2 in range(size)]
+    back = [(b, a) for a, b in pairs]
+    lower, upper = ([], [])
+    for step in range(size - 1):
+        if step % 2 == 0:
+            lower.append(lax.ppermute(lower[-1] if lower else hidden, "blk", pairs))
+        else:
+            upper.append(lax.ppermute(upper[-1] if upper else hidden, "blk", back))
+    pieces = jnp.stack([*lower[::-1], hidden, *upper])
+    shift = lax.axis_index("blk") - len(lower)
+    pieces = pieces[(jnp.arange(size) - shift) % size]
+    group_hidden = laid_out(pieces, 0)
     group_goal = lax.all_gather(targets, "blk", axis=0, tiled=True)
     owner_dev = group_goal // local_words
     in_group = owner_dev % blocks == group_idx

time: 274 us -> 274 us (level)
  blocking collectives: 25.8 us -> 8.23 us
  waiting for transfers between devices: 60.3 us -> 69.9 us
  starting transfers between devices: 11.7 us -> 18.5 us
    all_gather x1 -> x0, blocking collectives: 15.9 us -> none  [per_device(): group_hidden = lax.all_gather(hidden, 'blk', axis=0, tiled=True)]
    ppermute x0 -> x3, starting transfers between devices: none -> 7.35 us  [the longest x1 5.1 us: per_device(): upper.append(lax.ppermute(upper[-1] if upper else hidden, 'blk', back))]
    ppermute x0 -> x3, waiting for transfers between devices: none -> 4.72 us  [the longest x2 4.72 us: per_device(): lower.append(lax.ppermute(lower[-1] if lower else hidden, 'blk', pairs))]
    all_gather x1, waiting for transfers between devices: 29.1 us -> 33 us  [per_device(): word_panel = lax.all_gather(embeds, 'vocab', axis=0, tiled=True)]
  transfers between devices with their start and end apart: 17 -> 20, of which waited for: 9 -> 10; matrix products, arithmetic and copies ran while one was open for 19% -> 20% of each run, Pallas kernels for 0% -> 0%
where the time goes in v1:
time: 274 us; the launch traced here: 273 us
  matrix products  76.8 us (28%)
  local copies, waits for them, and re-layouts  74.6 us (27%)
  waiting for transfers between devices  69.9 us (26%)
  starting transfers between devices  18.5 us (7%)
  between operations  15 us (5%)
  other arithmetic  9.73 us (4%)
  blocking collectives  8.23 us (3%)
    all_gather x1, waiting for transfers between devices, per_device(): word_panel = lax.all_gather(embeds, 'vocab', axis=0, tiled=True)  33 us
    ppermute x16, waiting for transfers between devices, shifted(): lax.ppermute(array, axis, [(i, (i + by) % count) for i in range(count)])  32.1 us
    while x64, local copies, waits for them, and re-layouts  22.7 us
    gather x4, local copies, waits for them, and re-layouts, pick_targets(): jnp.take(word_panel, jnp.clip(row_spot, 0, count_words - 1), axis=0)  21 us
    dot_general x4, matrix products, char_features(): jnp.dot(windows.reshape(num_words * length, widths * embed_dim), masked,...  19.3 us
    slice x28, local copies, waits for them, and re-layouts, char_features(): padded[:, shift_at:shift_at + length, :]  17.9 us
    dot_general x4, matrix products, fold_panel(): lax.dot_general(row_block, word_panel, (((1,), (1,)), ((), ())), preferre...  17.1 us
    dot_general x4, matrix products, char_features(): jnp.dot(onehot.reshape(num_words * length, symbols), char_table, preferre...  16.7 us
  transfers between devices with their start and end apart: 20, of which 10 were waited for; matrix products, arithmetic and copies ran while one was open for 20% of the time, Pallas kernels for 0%

profile of v1, /device:TPU:0, one launch (start us, length us, event | category | flops | bytes accessed | tf_op | source)
XLA Modules:
  0.0 273.4 jit_solution(16857890084240592632)
XLA Ops:
  7.2 1.0 copy.20
  8.3 100.6 %while.13 = (s32[]{:T(128)}, bf16[4,128,1024]{2,1,0:T(8,128)(2,1)}, s32[4,128,50]{2,1,0:T(8,128)S(1)}, bf16[256,16]{0,1:T(8,128)(2,1)}, bf16[112,896]{1,0:T(8,12...) while((s32[]{:T(128)}, bf16[4,128,1024]{2,1,0:T(8,128)(2,1)}, ...), condition=%wide.region_2.3_spmd, body=%wide.region_0.2_spmd.sunk | while | flops 2662044928 | bytes 67010176 | solution.py:83
  8.5 4.2 %convolution_convert_fusion.4 = bf16[6400,16]{0,1:T(8,128)(2,1)S(1)} fusion(bf16[256,16]{0,1:T(8,128)(2,1)} %get-tuple-element.308, s32[6400]{0:T(1024)S(1)} %eq.55), kind=kOutput, calls=%fused_computation.6.clone.1 | convolution fusion | flops 54169600 | bytes 238592 | tf_op jit(solution)/shard_map/while/body/eval_jaxpr/dot_general | solution.py:29
  12.7 1.5 concatenate.12
  15.2 1.7 pad_slice_fusion.7
  16.8 1.4 copy.29
  24.1 4.8 %select_reduce_fusion.2 = f32[128,896]{1,0:T(8,128)S(1)} fusion(pred[50,896]{1,0:T(8,128)(4,1)S(1)} %iota_compare_fusion.6, bf16[128,50,112]{0,2,1:T(8,128)(2,1)} %constant_dynamic-update-slice_fusion.20, bf16[112,896]{1,0:T(8,128)(2,1)S(1)} %copy-done.9, s32[896]{0:T(1024)S(1)} %fusion.152, s32[112]{0:T(128)S(1)} %and_select_fusion.7), kind=kOutput, calls=%fused_computation.5.clone.1 | convolution fusion | flops 1296060416 | bytes 2141888 | tf_op jit(solution)/shard_map/while/body/eval_jaxpr/dot_general | solution.py:40
  30.0 1.2 copy-done.8
  32.2 1.2 fusion.157
  33.6 4.2 %convolution_convert_fusion.4 = bf16[6400,16]{0,1:T(8,128)(2,1)S(1)} fusion(bf16[256,16]{0,1:T(8,128)(2,1)} %get-tuple-element.308, s32[6400]{0:T(1024)S(1)} %eq.55), kind=kOutput, calls=%fused_computation.6.clone.1 | convolution fusion | flops 54169600 | bytes 238592 | tf_op jit(solution)/shard_map/while/body/eval_jaxpr/dot_general | solution.py:29
  37.8 1.5 concatenate.12
  40.3 1.7 pad_slice_fusion.7
  42.0 1.4 copy.29
  49.3 4.8 %select_reduce_fusion.2 = f32[128,896]{1,0:T(8,128)S(1)} fusion(pred[50,896]{1,0:T(8,128)(4,1)S(1)} %iota_compare_fusion.6, bf16[128,50,112]{0,2,1:T(8,128)(2,1)} %constant_dynamic-update-slice_fusion.20, bf16[112,896]{1,0:T(8,128)(2,1)S(1)} %copy-done.9, s32[896]{0:T(1024)S(1)} %fusion.152, s32[112]{0:T(128)S(1)} %and_select_fusion.7), kind=kOutput, calls=%fused_computation.5.clone.1 | convolution fusion | flops 1296060416 | bytes 2141888 | tf_op jit(solution)/shard_map/while/body/eval_jaxpr/dot_general | solution.py:40
  55.1 1.2 copy-done.8
  57.4 1.2 fusion.157
  58.8 4.2 %convolution_convert_fusion.4 = bf16[6400,16]{0,1:T(8,128)(2,1)S(1)} fusion(bf16[256,16]{0,1:T(8,128)(2,1)} %get-tuple-element.308, s32[6400]{0:T(1024)S(1)} %eq.55), kind=kOutput, calls=%fused_computation.6.clone.1 | convolution fusion | flops 54169600 | bytes 238592 | tf_op jit(solution)/shard_map/while/body/eval_jaxpr/dot_general | solution.py:29
  63.0 1.5 concatenate.12
  65.5 1.7 pad_slice_fusion.7
  67.2 1.4 copy.29
  74.4 4.8 %select_reduce_fusion.2 = f32[128,896]{1,0:T(8,128)S(1)} fusion(pred[50,896]{1,0:T(8,128)(4,1)S(1)} %iota_compare_fusion.6, bf16[128,50,112]{0,2,1:T(8,128)(2,1)} %constant_dynamic-update-slice_fusion.20, bf16[112,896]{1,0:T(8,128)(2,1)S(1)} %copy-done.9, s32[896]{0:T(1024)S(1)} %fusion.152, s32[112]{0:T(128)S(1)} %and_select_fusion.7), kind=kOutput, calls=%fused_computation.5.clone.1 | convolution fusion | flops 1296060416 | bytes 2141888 | tf_op jit(solution)/shard_map/while/body/eval_jaxpr/dot_general | solution.py:40
  80.3 1.2 copy-done.8
  82.5 1.3 fusion.157
  84.0 4.2 %convolution_convert_fusion.4 = bf16[6400,16]{0,1:T(8,128)(2,1)S(1)} fusion(bf16[256,16]{0,1:T(8,128)(2,1)} %get-tuple-element.308, s32[6400]{0:T(1024)S(1)} %eq.55), kind=kOutput, calls=%fused_computation.6.clone.1 | convolution fusion | flops 54169600 | bytes 238592 | tf_op jit(solution)/shard_map/while/body/eval_jaxpr/dot_general | solution.py:29
  88.2 1.5 concatenate.12
  90.7 1.7 pad_slice_fusion.7
  92.3 1.4 copy.29
  99.6 4.8 %select_reduce_fusion.2 = f32[128,896]{1,0:T(8,128)S(1)} fusion(pred[50,896]{1,0:T(8,128)(4,1)S(1)} %iota_compare_fusion.6, bf16[128,50,112]{0,2,1:T(8,128)(2,1)} %constant_dynamic-update-slice_fusion.20, bf16[112,896]{1,0:T(8,128)(2,1)S(1)} %copy-done.9, s32[896]{0:T(1024)S(1)} %fusion.152, s32[112]{0:T(128)S(1)} %and_select_fusion.7), kind=kOutput, calls=%fused_computation.5.clone.1 | convolution fusion | flops 1296060416 | bytes 2141888 | tf_op jit(solution)/shard_map/while/body/eval_jaxpr/dot_general | solution.py:40
  105.5 1.2 copy-done.8
  107.7 1.2 fusion.157
  108.9 5.1 %collective-permute-start.2 = (bf16[64,1024]{1,0:T(8,128)(2,1)}, bf16[64,1024]{1,0:T(8,128)(2,1)S(1)}, u32[]{:S(2)}, u32[]{:S(2)}) collective-permute-start(bf16[64,1024]{1,0:T(8,128)(2,1)} %param.20), channel_id=1, source_target_pairs={{1,0},{2,1},{3,2},{0,3},{5,4},{6,5},{7,6},{4,7},{9,8},{10,9},{11,1... | collective-permute-start | bytes 393224 | tf_op jit(solution)/shard_map/ppermute | solution.py:146
  115.6 8.2 %all-reduce.1 = s32[256]{0:T(256)S(1)} all-reduce(s32[256]{0:T(256)S(1)} %dynamic-update-slice), channel_id=1, replica_groups=mesh['vocab'=8,'blk'=4] {'blk'}, use_global_device_ids=true, to_apply=%add.1 | all-reduce | flops 256 | bytes 2048
  124.6 2.2 collective-permute-start.1
  126.9 4.7 %collective-permute-done.1 = bf16[64,1024]{1,0:T(8,128)(2,1)S(1)} collective-permute-done((bf16[64,1024]{1,0:T(8,128)(2,1)S(1)}, bf16[64,1024]{1,0:T(8,128)(2,1)S(1)}, u32[]{:S(2)}, u32[]{:S(2)}) %collective-permute-start.1) | collective-permute-done | bytes 131104 | tf_op jit(solution)/shard_map/ppermute | solution.py:144
  131.6 1.0 pad_maximum_fusion
  133.1 33.0 %all-gather.2.cloned.1.call-done = bf16[4096,1024]{1,0:T(8,128)(2,1)} async-done(((bf16[512,1024]{1,0:T(8,128)(2,1)}), bf16[4096,1024]{1,0:T(8,128)(2,1)}) %all-gather.2.cloned.1.call-update) | async-done | bytes 8388624 | tf_op jit(solution)/shard_map/all_gather | solution.py:137
  166.2 5.3 %gather_fusion.1 = bf16[64,1024]{1,0:T(8,128)(2,1)S(1)} fusion(bf16[4096,1024]{1,0:T(8,128)(2,1)} %all-gather.2.cloned.1.call-done, s32[1024]{0:T(1024)S(1)} %pad_clamp_fusion.3), kind=kCustom, calls=%fused_computation.clone | custom fusion | bytes 262400 | tf_op jit(solution)/shard_map/jit(_take)/gather | solution.py:89
  172.3 1.5 collective-permute-start.11
  173.7 6.3 %fusion.103 = (f32[64]{0:T(128)S(1)}, f32[64,4096]{1,0:T(8,128)S(1)}) fusion(bf16[4096,1024]{1,0:T(8,128)(2,1)} %all-gather.2.cloned.1.call-done, bf16[256,1024]{1,0:T(8,128)(2,1)S(1)} %bitcast.120, s32[]{:T(128)S(6)} %select_n.153), kind=kOutput, calls=%fused_computation.156 | convolution fusion | flops 537132992 | bytes 9568516 | tf_op jit(solution)/shard_map/dot_general | solution.py:97
  180.0 1.5 collective-permute-start.3
  182.4 2.4 convolution_add_fusion
  184.8 1.5 collective-permute-start.15
  186.8 3.3 %fusion.104 = (f32[64]{0:T(128)}, f32[64,4096]{1,0:T(8,128)S(1)}) fusion(bf16[4096,1024]{1,0:T(8,128)(2,1)S(1)} %copy-done, bf16[256,1024]{1,0:T(8,128)(2,1)S(1)} %bitcast.121, s32[]{:T(128)S(6)} %select_n.155), kind=kOutput, calls=%fused_computation.157 | convolution fusion | flops 537132992 | bytes 9568516 | tf_op jit(solution)/shard_map/dot_general | solution.py:97
  190.0 3.3 %fusion.105 = (f32[64]{0:T(128)}, f32[64,4096]{1,0:T(8,128)S(1)}) fusion(bf16[4096,1024]{1,0:T(8,128)(2,1)S(1)} %copy-done, bf16[256,1024]{1,0:T(8,128)(2,1)S(1)} %bitcast.122, s32[]{:T(128)S(6)} %select_n.157), kind=kOutput, calls=%fused_computation.158 | convolution fusion | flops 537132992 | bytes 9568516 | tf_op jit(solution)/shard_map/dot_general | solution.py:97
  193.4 4.2 %fusion.106 = (f32[64]{0:T(128)}, f32[64,4096]{1,0:T(8,128)S(1)}) fusion(bf16[4096,1024]{1,0:T(8,128)(2,1)S(1)} %copy-done, bf16[256,1024]{1,0:T(8,128)(2,1)} %bitcast.123, s32[]{:T(128)S(6)} %select_n.159), kind=kOutput, calls=%fused_computation.159 | convolution fusion | flops 537132992 | bytes 9568516 | tf_op jit(solution)/shard_map/dot_general | solution.py:97
  197.6 5.3 %gather_fusion.2 = bf16[64,1024]{1,0:T(8,128)(2,1)S(1)} fusion(bf16[4096,1024]{1,0:T(8,128)(2,1)} %all-gather.2.cloned.1.call-done, s32[1024]{0:T(1024)S(1)} %pad_clamp_fusion.2), kind=kCustom, calls=%fused_computation.1.clone | custom fusion | bytes 262400 | tf_op jit(solution)/shard_map/jit(_take)/gather | solution.py:89
  202.8 5.3 %gather_fusion.3 = bf16[64,1024]{1,0:T(8,128)(2,1)S(1)} fusion(bf16[4096,1024]{1,0:T(8,128)(2,1)} %all-gather.2.cloned.1.call-done, s32[1024]{0:T(1024)S(1)} %pad_clamp_fusion.1), kind=kCustom, calls=%fused_computation.2.clone | custom fusion | bytes 262400 | tf_op jit(solution)/shard_map/jit(_take)/gather | solution.py:89
  208.1 5.3 %gather_fusion.4 = bf16[64,1024]{1,0:T(8,128)(2,1)S(1)} fusion(bf16[4096,1024]{1,0:T(8,128)(2,1)} %all-gather.2.cloned.1.call-done, s32[1024]{0:T(1024)S(1)} %pad_clamp_fusion), kind=kCustom, calls=%fused_computation.3.clone | custom fusion | bytes 262400 | tf_op jit(solution)/shard_map/jit(_take)/gather | solution.py:89
  214.0 1.5 collective-permute-start.4
  216.4 1.5 collective-permute-start.8
  217.9 1.4 collective-permute-done.4
  220.4 1.4 collective-permute-done.8
  221.8 3.6 %collective-permute-done.5 = f32[64]{0:T(128)S(1)} collective-permute-done((f32[64]{0:T(128)S(1)}, f32[64]{0:T(128)S(1)}, u32[]{:S(2)}, u32[]{:S(2)}) %collective-permute-start.5) | collective-permute-done | bytes 288 | tf_op jit(solution)/shard_map/ppermute | solution.py:16
  225.9 1.1 select_add_fusion.2
  227.3 5.2 %multiply_add_fusion.2 = f32[64,1024]{1,0:T(8,128)S(1)} fusion(f32[64,1024]{1,0:T(8,128)} %collective-permute-done.15, f32[64]{0:T(128)S(1)} %get-tuple-element.173, bf16[4096,1024]{1,0:T(8,128)(2,1)} %all-gather.2.cloned.1.call-done, f32[64,4096]{1,0:T(8,128)S(1)} %get-tuple-element.209, f32[64]{0:T(128)S(1)} %max.43), kind=kOutput, calls=%fused_computation.90 | convolution fusion | flops 537526272 | bytes 9961984 | tf_op jit(solution)/shard_map/dot_general | solution.py:104
  232.9 4.2 %collective-permute-done.12 = f32[64,1024]{1,0:T(8,128)S(1)} collective-permute-done((f32[64,1024]{1,0:T(8,128)S(1)}, f32[64,1024]{1,0:T(8,128)S(1)}, u32[]{:S(2)}, u32[]{:S(2)}) %collective-permute-start.12) | collective-permute-done | bytes 262176 | tf_op jit(solution)/shard_map/ppermute | solution.py:16
  237.3 6.3 %collective-permute-done.16 = f32[64,1024]{1,0:T(8,128)S(1)} collective-permute-done((f32[64,1024]{1,0:T(8,128)S(1)}, f32[64,1024]{1,0:T(8,128)S(1)}, u32[]{:S(2)}, u32[]{:S(2)}) %collective-permute-start.16) | collective-permute-done | bytes 262176 | tf_op jit(solution)/shard_map/ppermute | solution.py:16
  243.6 1.7 multiply_add_fusion.1
  245.4 3.1 %collective-permute-done.13 = f32[64,1024]{1,0:T(8,128)S(1)} collective-permute-done((f32[64,1024]{1,0:T(8,128)S(1)}, f32[64,1024]{1,0:T(8,128)S(1)}, u32[]{:S(2)}, u32[]{:S(2)}) %collective-permute-start.13) | collective-permute-done | bytes 262176 | tf_op jit(solution)/shard_map/ppermute | solution.py:16
  248.7 6.4 %collective-permute-done.17 = f32[64,1024]{1,0:T(8,128)S(1)} collective-permute-done((f32[64,1024]{1,0:T(8,128)S(1)}, f32[64,1024]{1,0:T(8,128)S(1)}, u32[]{:S(2)}, u32[]{:S(2)}) %collective-permute-start.17) | collective-permute-done | bytes 262176 | tf_op jit(solution)/shard_map/ppermute | solution.py:16
  255.1 1.7 multiply_add_fusion
  257.0 2.4 collective-permute-start.6
  259.4 5.7 %collective-permute-done.10 = f32[64]{0:T(128)S(1)} collective-permute-done((f32[64]{0:T(128)S(1)}, f32[64]{0:T(128)S(1)}, u32[]{:S(2)}, u32[]{:S(2)}) %collective-permute-start.10) | collective-permute-done | bytes 288 | tf_op jit(solution)/shard_map/ppermute | solution.py:16
  265.1 0.9 subtract_convert_fusion
  (202 shorter events, 45.7 us)
Async XLA Ops:
  7.2 159.0 %all-gather.2.cloned.1.call-start = ((), (), s32[]{:S(2)}) async-start(), calls=%async_computation | async-start | bytes 9437184 | tf_op jit(solution)/shard_map/all_gather | solution.py:137
  8.2 105.8 %copy-start.11 = (u32[32]{0:T(128)S(1)}, u32[32]{0:T(128)}, u32[]{:S(2)}) copy-start(u32[32]{0:T(128)} %constant.234) | copy-start | bytes 388
  8.3 107.1 %copy-start.10 = (s32[64]{0:T(128)S(1)}, s32[64]{0:T(128)}, u32[]{:S(2)}) copy-start(s32[64]{0:T(128)} %param.21) | copy-start | bytes 772
  16.8 7.3 %copy-start.9 = (bf16[112,896]{1,0:T(8,128)(2,1)S(1)}, bf16[112,896]{1,0:T(8,128)(2,1)}, u32[]{:S(2)}) copy-start(bf16[112,896]{1,0:T(8,128)(2,1)} %get-tuple-element.309) | copy-start | bytes 602116 | tf_op jit(solution)/shard_map/while
  24.1 4.9 %copy-start.1 = (bf16[896,1024]{1,0:T(8,128)(2,1)S(1)}, bf16[896,1024]{1,0:T(8,128)(2,1)}, u32[]{:S(2)}) copy-start(bf16[896,1024]{1,0:T(8,128)(2,1)} %get-tuple-element.310) | copy-start | bytes 5505028 | tf_op jit(solution)/shard_map/while
  24.1 5.3 %copy-start.4 = (f32[2,1024]{1,0:T(2,128)S(1)}, f32[2,1024]{1,0:T(2,128)}, u32[]{:S(2)}) copy-start(f32[2,1024]{1,0:T(2,128)} %get-tuple-element.312) | copy-start | bytes 24580 | tf_op jit(solution)/shard_map/while
  24.1 5.3 %copy-start.7 = (bf16[2,1024,1024]{2,1,0:T(8,128)(2,1)S(1)}, bf16[2,1024,1024]{2,1,0:T(8,128)(2,1)}, u32[]{:S(2)}) copy-start(bf16[2,1024,1024]{2,1,0:T(8,128)(2,1)} %get-tuple-element.311) | copy-start | bytes 12582916 | tf_op jit(solution)/shard_map/while
  29.0 2.2 copy-start.8
  42.0 7.3 %copy-start.9 = (bf16[112,896]{1,0:T(8,128)(2,1)S(1)}, bf16[112,896]{1,0:T(8,128)(2,1)}, u32[]{:S(2)}) copy-start(bf16[112,896]{1,0:T(8,128)(2,1)} %get-tuple-element.309) | copy-start | bytes 602116 | tf_op jit(solution)/shard_map/while
  49.3 4.9 %copy-start.1 = (bf16[896,1024]{1,0:T(8,128)(2,1)S(1)}, bf16[896,1024]{1,0:T(8,128)(2,1)}, u32[]{:S(2)}) copy-start(bf16[896,1024]{1,0:T(8,128)(2,1)} %get-tuple-element.310) | copy-start | bytes 5505028 | tf_op jit(solution)/shard_map/while
  49.3 5.3 %copy-start.4 = (f32[2,1024]{1,0:T(2,128)S(1)}, f32[2,1024]{1,0:T(2,128)}, u32[]{:S(2)}) copy-start(f32[2,1024]{1,0:T(2,128)} %get-tuple-element.312) | copy-start | bytes 24580 | tf_op jit(solution)/shard_map/while
  49.3 5.3 %copy-start.7 = (bf16[2,1024,1024]{2,1,0:T(8,128)(2,1)S(1)}, bf16[2,1024,1024]{2,1,0:T(8,128)(2,1)}, u32[]{:S(2)}) copy-start(bf16[2,1024,1024]{2,1,0:T(8,128)(2,1)} %get-tuple-element.311) | copy-start | bytes 12582916 | tf_op jit(solution)/shard_map/while
  54.1 2.2 copy-start.8
  67.1 7.3 %copy-start.9 = (bf16[112,896]{1,0:T(8,128)(2,1)S(1)}, bf16[112,896]{1,0:T(8,128)(2,1)}, u32[]{:S(2)}) copy-start(bf16[112,896]{1,0:T(8,128)(2,1)} %get-tuple-element.309) | copy-start | bytes 602116 | tf_op jit(solution)/shard_map/while
  74.4 4.9 %copy-start.1 = (bf16[896,1024]{1,0:T(8,128)(2,1)S(1)}, bf16[896,1024]{1,0:T(8,128)(2,1)}, u32[]{:S(2)}) copy-start(bf16[896,1024]{1,0:T(8,128)(2,1)} %get-tuple-element.310) | copy-start | bytes 5505028 | tf_op jit(solution)/shard_map/while
  74.4 5.3 %copy-start.4 = (f32[2,1024]{1,0:T(2,128)S(1)}, f32[2,1024]{1,0:T(2,128)}, u32[]{:S(2)}) copy-start(f32[2,1024]{1,0:T(2,128)} %get-tuple-element.312) | copy-start | bytes 24580 | tf_op jit(solution)/shard_map/while
  74.4 5.3 %copy-start.7 = (bf16[2,1024,1024]{2,1,0:T(8,128)(2,1)S(1)}, bf16[2,1024,1024]{2,1,0:T(8,128)(2,1)}, u32[]{:S(2)}) copy-start(bf16[2,1024,1024]{2,1,0:T(8,128)(2,1)} %get-tuple-element.311) | copy-start | bytes 12582916 | tf_op jit(solution)/shard_map/while
  79.3 2.2 copy-start.8
  92.3 7.3 %copy-start.9 = (bf16[112,896]{1,0:T(8,128)(2,1)S(1)}, bf16[112,896]{1,0:T(8,128)(2,1)}, u32[]{:S(2)}) copy-start(bf16[112,896]{1,0:T(8,128)(2,1)} %get-tuple-element.309) | copy-start | bytes 602116 | tf_op jit(solution)/shard_map/while
  99.6 4.9 %copy-start.1 = (bf16[896,1024]{1,0:T(8,128)(2,1)S(1)}, bf16[896,1024]{1,0:T(8,128)(2,1)}, u32[]{:S(2)}) copy-start(bf16[896,1024]{1,0:T(8,128)(2,1)} %get-tuple-element.310) | copy-start | bytes 5505028 | tf_op jit(solution)/shard_map/while
  99.6 5.3 %copy-start.4 = (f32[2,1024]{1,0:T(2,128)S(1)}, f32[2,1024]{1,0:T(2,128)}, u32[]{:S(2)}) copy-start(f32[2,1024]{1,0:T(2,128)} %get-tuple-element.312) | copy-start | bytes 24580 | tf_op jit(solution)/shard_map/while
  99.6 5.3 %copy-start.7 = (bf16[2,1024,1024]{2,1,0:T(8,128)(2,1)S(1)}, bf16[2,1024,1024]{2,1,0:T(8,128)(2,1)}, u32[]{:S(2)}) copy-start(bf16[2,1024,1024]{2,1,0:T(8,128)(2,1)} %get-tuple-element.311) | copy-start | bytes 12582916 | tf_op jit(solution)/shard_map/while
  104.5 2.2 copy-start.8
  108.9 17.9 %collective-permute-start.2 = (bf16[64,1024]{1,0:T(8,128)(2,1)}, bf16[64,1024]{1,0:T(8,128)(2,1)S(1)}, u32[]{:S(2)}, u32[]{:S(2)}) collective-permute-start(bf16[64,1024]{1,0:T(8,128)(2,1)} %param.20), channel_id=1, source_target_pairs={{1,0},{2,1},{3,2},{0,3},{5,4},{6,5},{7,6},{4,7},{9,8},{10,9},{11,1... | collective-permute-start | bytes 393224 | tf_op jit(solution)/shard_map/ppermute | solution.py:146
  114.0 10.5 %collective-permute-start = (bf16[64,1024]{1,0:T(8,128)(2,1)}, bf16[64,1024]{1,0:T(8,128)(2,1)S(1)}, u32[]{:S(2)}, u32[]{:S(2)}) collective-permute-start(bf16[64,1024]{1,0:T(8,128)(2,1)} %param.20), channel_id=1, source_target_pairs={{0,1},{1,2},{2,3},{3,0},{4,5},{5,6},{6,7},{7,4},{8,9},{9,10},{10,1... | collective-permute-start | bytes 393224 | tf_op jit(solution)/shard_map/ppermute | solution.py:144
  124.6 7.0 %collective-permute-start.1 = (bf16[64,1024]{1,0:T(8,128)(2,1)S(1)}, bf16[64,1024]{1,0:T(8,128)(2,1)S(1)}, u32[]{:S(2)}, u32[]{:S(2)}) collective-permute-start(bf16[64,1024]{1,0:T(8,128)(2,1)S(1)} %collective-permute-done), channel_id=1, source_target_pairs={{0,1},{1,2},{2,3},{3,0},{4,5},{5,6},{6,7},{7,4},{8,9},{9,10},{10,1... | collective-permute-start | bytes 393224 | tf_op jit(solution)/shard_map/ppermute | solution.py:144
  133.1 56.9 %copy-start.2 = (bf16[4,64,1024]{2,1,0:T(8,128)(2,1)}, bf16[4,64,1024]{2,1,0:T(8,128)(2,1)S(1)}, u32[]{:S(2)}) copy-start(bf16[4,64,1024]{2,1,0:T(8,128)(2,1)S(1)} %gather_fusion) | copy-start | bytes 1572868
  172.3 53.7 %collective-permute-start.11 = (f32[64,1024]{1,0:T(8,128)}, f32[64,1024]{1,0:T(8,128)}, u32[]{:S(2)}, u32[]{:S(2)}) collective-permute-start(f32[64,1024]{1,0:T(8,128)} %convert_select_fusion), channel_id=1, source_target_pairs={{0,1},{1,2},{2,3},{3,0},{4,5},{5,6},{6,7},{7,4},{8,9},{9,10},{10,1... | collective-permute-start | bytes 786440 | tf_op jit(solution)/shard_map/ppermute | solution.py:16
  173.7 8.6 %copy-start = (bf16[4096,1024]{1,0:T(8,128)(2,1)S(1)}, bf16[4096,1024]{1,0:T(8,128)(2,1)}, u32[]{:S(2)}) copy-start(bf16[4096,1024]{1,0:T(8,128)(2,1)} %all-gather.2.cloned.1.call-done) | copy-start | bytes 25165828
  180.0 33.3 %collective-permute-start.3 = (f32[64]{0:T(128)S(1)}, f32[64]{0:T(128)}, u32[]{:S(2)}, u32[]{:S(2)}) collective-permute-start(f32[64]{0:T(128)S(1)} %get-tuple-element.206), channel_id=1, source_target_pairs={{0,1},{1,2},{2,3},{3,0},{4,5},{5,6},{6,7},{7,4},{8,9},{9,10},{10,1... | collective-permute-start | bytes 776 | tf_op jit(solution)/shard_map/ppermute | solution.py:16
  184.8 42.5 %collective-permute-start.15 = (f32[64,1024]{1,0:T(8,128)}, f32[64,1024]{1,0:T(8,128)}, u32[]{:S(2)}, u32[]{:S(2)}) collective-permute-start(f32[64,1024]{1,0:T(8,128)} %convolution_add_fusion), channel_id=1, source_target_pairs={{0,1},{1,2},{2,3},{3,0},{4,5},{5,6},{6,7},{7,4},{8,9},{9,10},{10,1... | collective-permute-start | bytes 786440 | tf_op jit(solution)/shard_map/ppermute | solution.py:16
  186.3 29.5 %collective-permute-start.7 = (f32[64]{0:T(128)}, f32[64]{0:T(128)}, u32[]{:S(2)}, u32[]{:S(2)}) collective-permute-start(f32[64]{0:T(128)} %get-tuple-element.205), channel_id=1, source_target_pairs={{0,1},{1,2},{2,3},{3,0},{4,5},{5,6},{6,7},{7,4},{8,9},{9,10},{10,1... | collective-permute-start | bytes 776 | tf_op jit(solution)/shard_map/ppermute | solution.py:16
  214.0 5.3 %collective-permute-start.4 = (f32[64]{0:T(128)S(1)}, f32[64]{0:T(128)S(1)}, u32[]{:S(2)}, u32[]{:S(2)}) collective-permute-start(f32[64]{0:T(128)S(1)} %max.43), channel_id=1, source_target_pairs={{0,1},{1,2},{2,3},{3,0},{4,5},{5,6},{6,7},{7,4},{8,9},{9,10},{10,1... | collective-permute-start | bytes 776 | tf_op jit(solution)/shard_map/ppermute | solution.py:16
  216.4 5.3 %collective-permute-start.8 = (f32[64]{0:T(128)S(1)}, f32[64]{0:T(128)S(1)}, u32[]{:S(2)}, u32[]{:S(2)}) collective-permute-start(f32[64]{0:T(128)S(1)} %get-tuple-element.172), channel_id=1, source_target_pairs={{0,1},{1,2},{2,3},{3,0},{4,5},{5,6},{6,7},{7,4},{8,9},{9,10},{10,1... | collective-permute-start | bytes 776 | tf_op jit(solution)/shard_map/ppermute | solution.py:16
  220.0 5.3 %collective-permute-start.5 = (f32[64]{0:T(128)S(1)}, f32[64]{0:T(128)S(1)}, u32[]{:S(2)}, u32[]{:S(2)}) collective-permute-start(f32[64]{0:T(128)S(1)} %max.44), channel_id=1, source_target_pairs={{0,1},{1,2},{2,3},{3,0},{4,5},{5,6},{6,7},{7,4},{8,9},{9,10},{10,1... | collective-permute-start | bytes 776 | tf_op jit(solution)/shard_map/ppermute | solution.py:16
  220.1 23.5 %slice-start = ((s8[8388608]{0:T(1024)(128)(4,1)}), s8[4194304]{0:T(1024)(128)(4,1)S(1)}, s32[]{:S(2)}) async-start(s8[8388608]{0:T(1024)(128)(4,1)} %bitcast.118), calls=%async_computation.1 | async-start | bytes 8388608
  221.8 23.6 %collective-permute-start.9 = (f32[64]{0:T(128)S(1)}, f32[64]{0:T(128)S(1)}, u32[]{:S(2)}, u32[]{:S(2)}) collective-permute-start(f32[64]{0:T(128)S(1)} %get-tuple-element.170), channel_id=1, source_target_pairs={{0,1},{1,2},{2,3},{3,0},{4,5},{5,6},{6,7},{7,4},{8,9},{9,10},{10,1... | collective-permute-start | bytes 776 | tf_op jit(solution)/shard_map/ppermute | solution.py:16
  227.0 10.1 %collective-permute-start.12 = (f32[64,1024]{1,0:T(8,128)S(1)}, f32[64,1024]{1,0:T(8,128)S(1)}, u32[]{:S(2)}, u32[]{:S(2)}) collective-permute-start(f32[64,1024]{1,0:T(8,128)S(1)} %select_add_fusion.2), channel_id=1, source_target_pairs={{0,1},{1,2},{2,3},{3,0},{4,5},{5,6},{6,7},{7,4},{8,9},{9,10},{10,1... | collective-permute-start | bytes 786440 | tf_op jit(solution)/shard_map/ppermute | solution.py:16
  227.3 9.8 %copy-start.5 = (pred[64]{0:T(512)(128)(4,1)S(1)}, pred[64]{0:T(512)(128)(4,1)}, u32[]{:S(2)}) copy-start(pred[64]{0:T(512)(128)(4,1)} %get-tuple-element.195) | copy-start | bytes 196
  227.3 9.8 %copy-start.6 = (pred[64]{0:T(512)(128)(4,1)S(1)}, pred[64]{0:T(512)(128)(4,1)}, u32[]{:S(2)}) copy-start(pred[64]{0:T(512)(128)(4,1)} %get-tuple-element.198) | copy-start | bytes 196
  227.3 16.3 %slice-start.1 = ((s8[8388608]{0:T(1024)(128)(4,1)}), s8[4194304]{0:T(1024)(128)(4,1)S(1)}, s32[]{:S(2)}) async-start(s8[8388608]{0:T(1024)(128)(4,1)} %bitcast.118), calls=%async_computation.2 | async-start | bytes 8388608
  232.5 11.1 %collective-permute-start.16 = (f32[64,1024]{1,0:T(8,128)S(1)}, f32[64,1024]{1,0:T(8,128)S(1)}, u32[]{:S(2)}, u32[]{:S(2)}) collective-permute-start(f32[64,1024]{1,0:T(8,128)S(1)} %multiply_add_fusion.2), channel_id=1, source_target_pairs={{0,1},{1,2},{2,3},{3,0},{4,5},{5,6},{6,7},{7,4},{8,9},{9,10},{10,1... | collective-permute-start | bytes 786440 | tf_op jit(solution)/shard_map/ppermute | solution.py:16
  237.2 11.3 %collective-permute-start.13 = (f32[64,1024]{1,0:T(8,128)S(1)}, f32[64,1024]{1,0:T(8,128)S(1)}, u32[]{:S(2)}, u32[]{:S(2)}) collective-permute-start(f32[64,1024]{1,0:T(8,128)S(1)} %select_add_fusion.1), channel_id=1, source_target_pairs={{0,1},{1,2},{2,3},{3,0},{4,5},{5,6},{6,7},{7,4},{8,9},{9,10},{10,1... | collective-permute-start | bytes 786440 | tf_op jit(solution)/shard_map/ppermute | solution.py:16
  245.3 9.8 %collective-permute-start.17 = (f32[64,1024]{1,0:T(8,128)S(1)}, f32[64,1024]{1,0:T(8,128)S(1)}, u32[]{:S(2)}, u32[]{:S(2)}) collective-permute-start(f32[64,1024]{1,0:T(8,128)S(1)} %multiply_add_fusion.1), channel_id=1, source_target_pairs={{0,1},{1,2},{2,3},{3,0},{4,5},{5,6},{6,7},{7,4},{8,9},{9,10},{10,1... | collective-permute-start | bytes 786440 | tf_op jit(solution)/shard_map/ppermute | solution.py:16
  248.6 16.5 %collective-permute-start.14 = (f32[64,1024]{1,0:T(8,128)S(1)}, f32[64,1024]{1,0:T(8,128)S(1)}, u32[]{:S(2)}, u32[]{:S(2)}) collective-permute-start(f32[64,1024]{1,0:T(8,128)S(1)} %select_add_fusion), channel_id=1, source_target_pairs={{0,1},{1,2},{2,3},{3,0},{4,5},{5,6},{6,7},{7,4},{8,9},{9,10},{10,1... | collective-permute-start | bytes 786440 | tf_op jit(solution)/shard_map/ppermute | solution.py:16
  255.1 10.0 %copy-start.3 = (bf16[64,1024]{1,0:T(8,128)(2,1)S(1)}, bf16[64,1024]{1,0:T(8,128)(2,1)}, u32[]{:S(2)}) copy-start(bf16[64,1024]{1,0:T(8,128)(2,1)} %param.20) | copy-start | bytes 393220
  256.8 8.3 %collective-permute-start.18 = (f32[64,1024]{1,0:T(8,128)S(1)}, f32[64,1024]{1,0:T(8,128)S(1)}, u32[]{:S(2)}, u32[]{:S(2)}) collective-permute-start(f32[64,1024]{1,0:T(8,128)S(1)} %multiply_add_fusion), channel_id=1, source_target_pairs={{0,1},{1,2},{2,3},{3,0},{4,5},{5,6},{6,7},{7,4},{8,9},{9,10},{10,1... | collective-permute-start | bytes 786440 | tf_op jit(solution)/shard_map/ppermute | solution.py:16
  256.9 8.2 %collective-permute-start.10 = (f32[64]{0:T(128)S(1)}, f32[64]{0:T(128)S(1)}, u32[]{:S(2)}, u32[]{:S(2)}) collective-permute-start(f32[64]{0:T(128)S(1)} %get-tuple-element.168), channel_id=1, source_target_pairs={{0,1},{1,2},{2,3},{3,0},{4,5},{5,6},{6,7},{7,4},{8,9},{9,10},{10,1... | collective-permute-start | bytes 776 | tf_op jit(solution)/shard_map/ppermute | solution.py:16
  257.0 9.0 %collective-permute-start.6 = (f32[64]{0:T(128)S(1)}, f32[64]{0:T(128)S(1)}, u32[]{:S(2)}, u32[]{:S(2)}) collective-permute-start(f32[64]{0:T(128)S(1)} %max.45), channel_id=1, source_target_pairs={{0,1},{1,2},{2,3},{3,0},{4,5},{5,6},{6,7},{7,4},{8,9},{9,10},{10,1... | collective-permute-start | bytes 776 | tf_op jit(solution)/shard_map/ppermute | solution.py:16
Sparse Core Ops, SparseCore 0:
  109.1 57.0 all-gather.1
